TPU v7x, 32 devices: a whole 2x2x4 slice. The times are simulated.
32 devices in a mesh: bank: 8 (over z, y), grp: 4 (over x, core).
Axes of the slice: x: 2, y: 2, z: 4, core: 2. Of those that a mesh axis runs over, the one named last changes fastest.
Arguments:
- users: bfloat16 [4096, 256], P(('bank', 'grp')), may hold values from -32 to 32
- bank: bfloat16 [4096, 256], P('bank'), may hold values from -3 to 3
- positives: int32 [4096], P(('bank', 'grp')), may hold values from 0 to 4095
- cohorts: int32 [4096], P(('bank', 'grp')), may hold values from 0 to 15
Outputs:
- loss: float32 [], replicated
- user_grad: float32 [4096, 256], P(('bank', 'grp'))
- bank_grad: float32 [4096, 256], P(('bank', 'grp'))
All inputs are finite; a program needn't handle non-finite values.
Results may differ from a plain program's by a relative error of at most 0.014.
Values may be sent and summed in bfloat16 or wider, within the bound.
A program may use at most 64 MiB of HBM per device.

v0:
```python
import jax
import jax.numpy as jnp
from jax import lax
from jax.sharding import PartitionSpec as P

NCOH = 16


def make_dlogits(upart, local_pos, weight, lse, bank):
    logits = jnp.dot(upart, bank.T, preferred_element_type=jnp.float32)
    item_ids = jnp.arange(bank.shape[0], dtype=jnp.int32)
    hot = (item_ids[None, :] == local_pos[:, None]).astype(jnp.float32)
    prob = jnp.exp(logits - lse[:, None])
    return (weight[:, None] * (prob - hot)).astype(jnp.bfloat16)


def per_device(users, bank, positives, cohorts):
    per_dev = users.shape[0]
    items_here = bank.shape[0]
    bank_size = lax.axis_size("bank")
    total_users = per_dev * bank_size * lax.axis_size("grp")
    cohort_ids = jnp.arange(NCOH, dtype=jnp.int32)
    local_counts = jnp.sum((cohorts[:, None] == cohort_ids[None, :]).astype(jnp.float32), axis=0)
    counts = lax.psum(local_counts, ("bank", "grp"))
    gathered, gpos, gcoh = (
        lax.all_gather(users, "bank", axis=0, tiled=True),
        lax.all_gather(positives, "bank", axis=0, tiled=True),
        lax.all_gather(cohorts, "bank", axis=0, tiled=True),
    )
    rows = gathered.shape[0]
    own = jnp.sum(
        jnp.where(gcoh[:, None] == cohort_ids[None, :], counts[None, :], jnp.float32(0.0)), axis=1
    )
    weight = jnp.float32(total_users) / NCOH / own
    local_pos = gpos - lax.axis_index("bank") * items_here
    block = 512
    count = rows // block
    ublocks = gathered.reshape(count, block, gathered.shape[1])
    pblocks = local_pos.reshape(count, block)
    item_ids = jnp.arange(items_here, dtype=jnp.int32)

    def forward(carry, parts):
        upart, ppart = parts
        logits = jnp.dot(upart, bank.T, preferred_element_type=jnp.float32)
        top = jnp.max(logits, axis=1)
        total = jnp.sum(jnp.exp(logits - top[:, None]), axis=1)
        pos_logit = jnp.sum(
            jnp.where(item_ids[None, :] == ppart[:, None], logits, jnp.float32(0.0)), axis=1
        )
        return (carry, (top, total, pos_logit))

    _, (top_loc, sum_loc, pos_loc) = lax.scan(forward, 0, (ublocks, pblocks))
    top_loc = top_loc.reshape(rows)
    sum_loc = sum_loc.reshape(rows)
    pos_loc = pos_loc.reshape(rows)
    top_all = lax.pmax(top_loc, "bank")
    sum_all = lax.psum(sum_loc * jnp.exp(top_loc - top_all), "bank")
    lse = top_all + jnp.log(sum_all)
    loss_part = jnp.sum(weight * lse) / jnp.float32(bank_size) - jnp.sum(weight * pos_loc)
    loss = lax.psum(loss_part, ("bank", "grp")) / jnp.float32(total_users)
    wblocks = weight.reshape(count, block)
    lblocks = lse.reshape(count, block)
    empty = jnp.zeros((items_here, gathered.shape[1]), jnp.float32)

    def backward(bacc, parts):
        upart, ppart, wpart, lpart = parts
        dlogits = make_dlogits(upart, ppart, wpart, lpart, bank)
        ugrad = jnp.dot(dlogits, bank, preferred_element_type=jnp.float32)
        bacc = bacc + lax.dot_general(
            dlogits, upart, (((0,), (0,)), ((), ())), preferred_element_type=jnp.float32
        )
        return (bacc, ugrad)

    bank_part, ugrads = lax.scan(backward, empty, (ublocks, pblocks, wblocks, lblocks))
    user_grad = lax.psum_scatter(
        ugrads.reshape(rows, gathered.shape[1]).astype(jnp.bfloat16),
        "bank",
        scatter_dimension=0,
        tiled=True,
    ).astype(jnp.float32)
    bank_grad = lax.psum_scatter(
        bank_part.astype(jnp.bfloat16), "grp", scatter_dimension=0, tiled=True
    ).astype(jnp.float32)
    return (loss, user_grad, bank_grad)


def solution(mesh):
    placed = (P(("bank", "grp"), None), P("bank", None), P(("bank", "grp")), P(("bank", "grp")))
    return jax.shard_map(
        per_device,
        mesh=mesh,
        in_specs=placed,
        out_specs=(P(), P(("bank", "grp"), None), P(("bank", "grp"), None)),
        check_vma=False,
    )
```

profile of v0, /device:TPU:0, one launch (start us, length us, event | category | flops | bytes accessed | tf_op | source)
XLA Modules:
  0.0 254.8 jit_solution(5209319706472410693)
XLA Ops:
  7.2 0.0 reduce-scatter.5.cloned.1.call-start
  7.2 0.0 copy-start.3
  7.3 0.6 copy-done.3
  7.9 0.1 convert_reduce_fusion
  8.0 42.0 %psum.21 = f32[16]{0:T(128)S(1)} all-reduce(f32[16]{0:T(128)S(1)} %convert_reduce_fusion), channel_id=1, replica_groups=mesh['bank'=8,'grp'=4] {'bank','grp'}, use_global_device_ids=true, to_apply=%region_1.0 | all-reduce | flops 16 | bytes 128 | tf_op jit(solution)/shard_map/psum | solution.py:24
  50.0 0.0 copy-start.2
  50.0 0.7 copy-done.2
  50.7 20.2 %all-gather.1 = s32[8,1,128]{2,1,0:T(1,128)S(1)} all-gather(s32[1,1,128]{2,1,0:T(1,128)S(1)} %bitcast.82), channel_id=1, replica_groups=mesh['bank'=8,'grp'=4] {'bank'}, dimensions={0}, use_global_device_ids=true | all-gather | bytes 4608 | tf_op jit(solution)/shard_map/all_gather | solution.py:27
  70.8 16.3 %all-gather = s32[8,1,128]{2,1,0:T(1,128)S(1)} all-gather(s32[1,1,128]{2,1,0:T(1,128)S(1)} %bitcast.83), channel_id=1, replica_groups=mesh['bank'=8,'grp'=4] {'bank'}, dimensions={0}, use_global_device_ids=true | all-gather | bytes 4608 | tf_op jit(solution)/shard_map/all_gather | solution.py:28
  87.1 0.0 copy-start
  87.1 31.5 %all_gather.10 = bf16[1024,256]{1,0:T(8,128)(2,1)S(1)} all-gather(bf16[128,256]{1,0:T(8,128)(2,1)} %param.8), channel_id=1, replica_groups=mesh['bank'=8,'grp'=4] {'bank'}, dimensions={0}, use_global_device_ids=true | all-gather | bytes 589824 | tf_op jit(solution)/shard_map/all_gather | solution.py:26
  118.7 0.0 copy-done
  118.7 1.6 while.28
  118.7 0.4 fusion.34
  119.0 0.3 select_reduce_fusion.3
  119.5 0.4 fusion.34
  119.8 0.3 select_reduce_fusion.3
  120.3 19.3 %pmax.7 = f32[1024]{0:T(1024)S(1)} all-reduce(f32[1024]{0:T(1024)S(1)} %bitcast.76), channel_id=1, replica_groups=mesh['bank'=8,'grp'=4] {'bank'}, use_global_device_ids=true, to_apply=%region_8.9 | all-reduce | flops 1024 | bytes 8192 | tf_op jit(solution)/shard_map/pmax | solution.py:56
  139.6 17.1 %psum.22 = f32[1024]{0:T(1024)S(1)} all-reduce(f32[1024]{0:T(1024)S(1)} %exponential_multiply_fusion), channel_id=1, replica_groups=mesh['bank'=8,'grp'=4] {'bank'}, use_global_device_ids=true, to_apply=%region_9.10 | all-reduce | flops 1024 | bytes 8192 | tf_op jit(solution)/shard_map/psum | solution.py:57
  156.7 0.1 select_reduce_fusion.1
  156.8 0.6 multiply_reduce_fusion.1
  157.4 2.5 while.29
  157.5 0.5 fusion.41
  157.9 0.4 convolution_add_fusion.2
  158.4 0.3 fusion.42
  158.7 0.5 fusion.41
  159.2 0.4 convolution_add_fusion.2
  159.7 0.3 fusion.42
  160.0 0.0 copy-start.1
  160.0 0.8 convert_element_type.28
  160.8 0.0 reduce-scatter.5.cloned.1.call-update
  160.8 0.0 copy-done.1
  160.8 0.0 reduce-scatter.3.cloned.1.call-start
  160.9 0.7 reduce-scatter.3.cloned.1.call-update
  162.2 0.6 multiply_reduce_fusion
  163.5 37.6 %psum.23 = f32[]{:T(128)} all-reduce(f32[]{:T(128)S(6)} %sub.36), channel_id=1, replica_groups=mesh['bank'=8,'grp'=4] {'bank','grp'}, use_global_device_ids=true, to_apply=%region_12.13 | all-reduce | flops 1 | bytes 8 | tf_op jit(solution)/shard_map/psum | solution.py:60
  201.7 0.0 reduce-scatter.5.cloned.1.call-done
  201.7 1.5 convert_element_type.29
  203.3 42.1 %reduce-scatter.3.cloned.1.call-done = bf16[128,256]{1,0:T(8,128)(2,1)} async-done(((bf16[1024,256]{1,0:T(8,128)(2,1)}), bf16[128,256]{1,0:T(8,128)(2,1)}) %reduce-scatter.3.cloned.1.call-update) | async-done | bytes 65552 | tf_op jit(solution)/shard_map/reduce_scatter | solution.py:75
  245.3 1.5 convert_element_type.27
  (24 shorter events, 0.4 us)
Async XLA Ops:
  7.2 194.6 %reduce-scatter.5.cloned.1.call-start = ((), (), s32[]{:S(2)}) async-start(), calls=%async_computation.3 | async-start | bytes 327680 | tf_op jit(solution)/shard_map/reduce_scatter | solution.py:81
  7.2 0.7 copy-start.3
  50.0 0.7 copy-start.2
  87.1 31.5 %copy-start = (bf16[512,256]{1,0:T(8,128)(2,1)S(1)}, bf16[512,256]{1,0:T(8,128)(2,1)}, u32[]{:S(2)}) copy-start(bf16[512,256]{1,0:T(8,128)(2,1)} %param.9) | copy-start | bytes 786436
  160.0 0.9 copy-start.1
  160.8 84.5 %reduce-scatter.3.cloned.1.call-start = ((), (), s32[]{:S(2)}) async-start(), calls=%async_computation.2 | async-start | bytes 589824 | tf_op jit(solution)/shard_map/reduce_scatter | solution.py:75
Sparse Core Ops, SparseCore 0:
  160.9 17.9 reduce-scatter.4
  182.3 62.9 reduce-scatter.2
where the time goes:
time: 255 us
  blocking collectives  184 us (72%)
  waiting for transfers between devices  42.8 us (17%)
  between operations  17.2 us (7%)
  other arithmetic  5.83 us (2%)
  matrix products  3.1 us (1%)
    reduce_scatter x1, waiting for transfers between devices, per_device(): lax.psum_scatter(ugrads.reshape(rows, gathered.shape[1]).astype(jnp.bfloa...  42.1 us
    psum x1, blocking collectives, per_device(): counts = lax.psum(local_counts, ('bank', 'grp'))  42 us
    psum x1, blocking collectives, per_device(): loss = lax.psum(loss_part, ('bank', 'grp')) / jnp.float32(total_users)  37.6 us
    all_gather x1, blocking collectives, per_device(): lax.all_gather(users, 'bank', axis=0, tiled=True)  31.5 us
    all_gather x1, blocking collectives, per_device(): lax.all_gather(positives, 'bank', axis=0, tiled=True)  20.2 us
    pmax x1, blocking collectives, per_device(): top_all = lax.pmax(top_loc, 'bank')  19.3 us
    psum x1, blocking collectives, per_device(): sum_all = lax.psum(sum_loc * jnp.exp(top_loc - top_all), 'bank')  17.1 us
    all_gather x1, blocking collectives, per_device(): lax.all_gather(cohorts, 'bank', axis=0, tiled=True)  16.3 us
  transfers between devices with their start and end apart: 2, of which 1 were waited for; matrix products, arithmetic and copies ran while one was open for 1% of the time, Pallas kernels for 0%

commit v1 on v0

--- a/solution.py
+++ b/solution.py
@@ -54,7 +54,7 @@
     sum_loc = sum_loc.reshape(rows)
     pos_loc = pos_loc.reshape(rows)
     top_all = lax.pmax(top_loc, "bank")
-    sum_all = lax.psum(sum_loc * jnp.exp(top_loc - top_all), "bank")
+    sum_all = jnp.sum(lax.all_gather(sum_loc * jnp.exp(top_loc - top_all), "bank"), axis=0)
     lse = top_all + jnp.log(sum_all)
     loss_part = jnp.sum(weight * lse) / jnp.float32(bank_size) - jnp.sum(weight * pos_loc)
     loss = lax.psum(loss_part, ("bank", "grp")) / jnp.float32(total_users)

time: 255 us -> 267 us (1.047)
  blocking collectives: 184 us -> 197 us
    all_gather x0 -> x1, blocking collectives: none -> 30.6 us  [per_device(): lax.all_gather(sum_loc * jnp.exp(top_loc - top_all), 'bank')]
    psum x1 -> x0, blocking collectives: 17.1 us -> none  [per_device(): sum_all = lax.psum(sum_loc * jnp.exp(top_loc - top_all), 'bank')]
where the time goes in v1:
time: 267 us
  blocking collectives  197 us (74%)
  waiting for transfers between devices  42 us (16%)
  between operations  17.2 us (6%)
  other arithmetic  5.84 us (2%)
  matrix products  3.11 us (1%)
    psum x1, blocking collectives, per_device(): counts = lax.psum(local_counts, ('bank', 'grp'))  42 us
    reduce_scatter x1, waiting for transfers between devices, per_device(): lax.psum_scatter(ugrads.reshape(rows, gathered.shape[1]).astype(jnp.bfloa...  41.2 us
    psum x1, blocking collectives, per_device(): loss = lax.psum(loss_part, ('bank', 'grp')) / jnp.float32(total_users)  37 us
    all_gather x1, blocking collectives, per_device(): lax.all_gather(users, 'bank', axis=0, tiled=True)  31.6 us
    all_gather x1, blocking collectives, per_device(): lax.all_gather(sum_loc * jnp.exp(top_loc - top_all), 'bank')  30.6 us
    all_gather x1, blocking collectives, per_device(): lax.all_gather(positives, 'bank', axis=0, tiled=True)  20.2 us
    pmax x1, blocking collectives, per_device(): top_all = lax.pmax(top_loc, 'bank')  19.2 us
    all_gather x1, blocking collectives, per_device(): lax.all_gather(cohorts, 'bank', axis=0, tiled=True)  16.3 us
  transfers between devices with their start and end apart: 2, of which 1 were waited for; matrix products, arithmetic and copies ran while one was open for 1% of the time, Pallas kernels for 0%

profile of v1, /device:TPU:0, one launch (start us, length us, event | category | flops | bytes accessed | tf_op | source)
XLA Modules:
  0.0 266.9 jit_solution(3384613876872401110)
XLA Ops:
  7.2 0.0 reduce-scatter.5.cloned.1.call-start
  7.2 0.0 copy-start.3
  7.3 0.6 copy-done.3
  7.9 0.1 convert_reduce_fusion
  8.0 42.0 %psum.14 = f32[16]{0:T(128)S(1)} all-reduce(f32[16]{0:T(128)S(1)} %convert_reduce_fusion), channel_id=1, replica_groups=mesh['bank'=8,'grp'=4] {'bank','grp'}, use_global_device_ids=true, to_apply=%region_1.0 | all-reduce | flops 16 | bytes 128 | tf_op jit(solution)/shard_map/psum | solution.py:24
  50.0 0.0 copy-start.2
  50.0 0.7 copy-done.2
  50.7 20.2 %all-gather.2 = s32[8,1,128]{2,1,0:T(1,128)S(1)} all-gather(s32[1,1,128]{2,1,0:T(1,128)S(1)} %bitcast.82), channel_id=1, replica_groups=mesh['bank'=8,'grp'=4] {'bank'}, dimensions={0}, use_global_device_ids=true | all-gather | bytes 4608 | tf_op jit(solution)/shard_map/all_gather | solution.py:27
  70.9 16.3 %all-gather.1 = s32[8,1,128]{2,1,0:T(1,128)S(1)} all-gather(s32[1,1,128]{2,1,0:T(1,128)S(1)} %bitcast.83), channel_id=1, replica_groups=mesh['bank'=8,'grp'=4] {'bank'}, dimensions={0}, use_global_device_ids=true | all-gather | bytes 4608 | tf_op jit(solution)/shard_map/all_gather | solution.py:28
  87.1 0.0 copy-start
  87.1 31.6 %all_gather.16 = bf16[1024,256]{1,0:T(8,128)(2,1)S(1)} all-gather(bf16[128,256]{1,0:T(8,128)(2,1)} %param.8), channel_id=1, replica_groups=mesh['bank'=8,'grp'=4] {'bank'}, dimensions={0}, use_global_device_ids=true | all-gather | bytes 589824 | tf_op jit(solution)/shard_map/all_gather | solution.py:26
  118.7 0.0 copy-done
  118.7 1.6 while.28
  118.7 0.4 fusion.34
  119.1 0.3 select_reduce_fusion.3
  119.5 0.4 fusion.34
  119.9 0.3 select_reduce_fusion.3
  120.3 19.2 %pmax.7 = f32[1024]{0:T(1024)S(1)} all-reduce(f32[1024]{0:T(1024)S(1)} %bitcast.76), channel_id=1, replica_groups=mesh['bank'=8,'grp'=4] {'bank'}, use_global_device_ids=true, to_apply=%region_8.9 | all-reduce | flops 1024 | bytes 8192 | tf_op jit(solution)/shard_map/pmax | solution.py:56
  139.6 30.6 %all-gather = f32[8192]{0:T(1024)S(1)} all-gather(f32[1024]{0:T(1024)S(1)} %exponential_multiply_fusion), channel_id=2, replica_groups=mesh['bank'=8,'grp'=4] {'bank'}, dimensions={0}, use_global_device_ids=true | all-gather | bytes 36864 | tf_op jit(solution)/shard_map/all_gather | solution.py:57
  170.2 0.1 select_reduce_fusion.1
  170.3 0.6 multiply_reduce_fusion.1
  170.9 2.5 while.29
  171.0 0.5 fusion.41
  171.4 0.4 convolution_add_fusion.2
  171.9 0.3 fusion.42
  172.2 0.5 fusion.41
  172.7 0.4 convolution_add_fusion.2
  173.2 0.3 fusion.42
  173.5 0.0 copy-start.1
  173.5 0.8 convert_element_type.28
  174.3 0.0 reduce-scatter.5.cloned.1.call-update
  174.3 0.0 copy-done.1
  174.3 0.0 reduce-scatter.3.cloned.1.call-start
  174.4 0.7 reduce-scatter.3.cloned.1.call-update
  175.7 0.6 multiply_reduce_fusion
  177.0 37.0 %psum.15 = f32[]{:T(128)} all-reduce(f32[]{:T(128)S(6)} %sub.36), channel_id=1, replica_groups=mesh['bank'=8,'grp'=4] {'bank','grp'}, use_global_device_ids=true, to_apply=%region_12.13 | all-reduce | flops 1 | bytes 8 | tf_op jit(solution)/shard_map/psum | solution.py:60
  214.6 0.0 reduce-scatter.5.cloned.1.call-done
  214.7 1.5 convert_element_type.29
  216.2 41.2 %reduce-scatter.3.cloned.1.call-done = bf16[128,256]{1,0:T(8,128)(2,1)} async-done(((bf16[1024,256]{1,0:T(8,128)(2,1)}), bf16[128,256]{1,0:T(8,128)(2,1)}) %reduce-scatter.3.cloned.1.call-update) | async-done | bytes 65552 | tf_op jit(solution)/shard_map/reduce_scatter | solution.py:75
  257.4 1.5 convert_element_type.27
  (26 shorter events, 0.4 us)
Async XLA Ops:
  7.2 207.5 %reduce-scatter.5.cloned.1.call-start = ((), (), s32[]{:S(2)}) async-start(), calls=%async_computation.3 | async-start | bytes 327680 | tf_op jit(solution)/shard_map/reduce_scatter | solution.py:81
  7.2 0.7 copy-start.3
  50.0 0.7 copy-start.2
  87.1 31.6 %copy-start = (bf16[512,256]{1,0:T(8,128)(2,1)S(1)}, bf16[512,256]{1,0:T(8,128)(2,1)}, u32[]{:S(2)}) copy-start(bf16[512,256]{1,0:T(8,128)(2,1)} %param.9) | copy-start | bytes 786436
  173.5 0.9 copy-start.1
  174.3 83.0 %reduce-scatter.3.cloned.1.call-start = ((), (), s32[]{:S(2)}) async-start(), calls=%async_computation.2 | async-start | bytes 589824 | tf_op jit(solution)/shard_map/reduce_scatter | solution.py:75
Sparse Core Ops, SparseCore 0:
  174.4 16.4 reduce-scatter.4
  194.2 63.1 reduce-scatter.2
